TPU v7x, 256 devices: a whole 4x4x8 slice. The times are simulated.
256 devices in a mesh: row: 16 (over z, core), col: 16 (over x, y).
Axes of the slice: x: 4, y: 4, z: 8, core: 2. Of those that a mesh axis runs over, the one named last changes fastest.
Arguments:
- panel: float32 [16384, 128], P(('row', 'col')), as said below
- mobility: float32 [16384, 16384], P('row', 'col'), as said below
Outputs:
- updated: float32 [16384, 16384], P('row', 'col')
- panel_factor: float32 [128, 128], replicated
Inputs may be any that keep to these rules, and one draw needn't show every extreme that they name: Each row and each column of the panel has its own scale. `mobility`: Symmetric.
All inputs are finite; a program needn't handle non-finite values.
Results may differ from a plain program's by a relative error of at most 0.000076.
Values sent between devices are 32-bit elements; how exact they have to be, the bound alone decides.
No kernel may reach another device: no remote copies, remote signals or barrier semaphores. Data moves between devices by JAX's collectives and lax.ppermute only.
A program may use at most 64 MiB of HBM per device.

v0:
```python
import jax
import jax.numpy as jnp
from jax import lax
from jax.sharding import PartitionSpec as P


def spread(shard, axis, root):
    mine = lax.axis_index(axis) == root
    return lax.psum(jnp.where(mine, shard, jnp.zeros_like(shard)), axis)


def product(first_op, second_op):
    return jnp.dot(
        first_op, second_op, precision=lax.Precision.HIGHEST, preferred_element_type=jnp.float32
    )


def product_tn(first_op, second_op):
    return lax.dot_general(
        first_op,
        second_op,
        (((0,), (0,)), ((), ())),
        precision=lax.Precision.HIGHEST,
        preferred_element_type=jnp.float32,
    )


def product_nt(first_op, second_op):
    return lax.dot_general(
        first_op,
        second_op,
        (((1,), (1,)), ((), ())),
        precision=lax.Precision.HIGHEST,
        preferred_element_type=jnp.float32,
    )


def invert_core(core_matrix):
    identity = jnp.eye(core_matrix.shape[0], dtype=jnp.float32)

    def newton_step(index, approx):
        return product(approx, 2.0 * identity - product(core_matrix, approx))

    return lax.fori_loop(0, 12, newton_step, identity)


def correction_columns(block_rows_arr, block_ratio):
    root_index = lax.axis_index("col") * block_ratio + 0
    copies = spread(block_rows_arr, "row", root_index)
    return copies


def on_device(panel, mobility):
    piece_rows = panel.shape[0]
    width_cols = panel.shape[1]
    count_col = lax.axis_size("col")
    count_row = lax.axis_size("row")
    block_ratio = count_row // count_col
    row_index = lax.axis_index("row")
    col_index = lax.axis_index("col")
    block_rows = mobility.shape[0]
    block_cols = mobility.shape[1]
    first_row = (row_index * count_col + col_index) * piece_rows
    positions = first_row + jnp.arange(piece_rows, dtype=jnp.int32)
    selector = (jnp.arange(width_cols, dtype=jnp.int32)[:, None] == positions[None, :]).astype(
        jnp.float32
    )
    gram_term = product_tn(panel, panel)
    top_term = product(selector, panel)
    gram_sum, top_rows = lax.psum((gram_term, top_term), ("row", "col"))
    lower_factor = jnp.linalg.cholesky(gram_sum)
    panel_factor = lower_factor.T
    ortho_piece = jax.scipy.linalg.solve_triangular(lower_factor, panel.T, lower=True).T
    basis_piece = ortho_piece + selector.T
    top_ortho = jax.scipy.linalg.solve_triangular(lower_factor, top_rows.T, lower=True)
    core_matrix = jnp.eye(width_cols, dtype=jnp.float32) + top_ortho
    kernel = invert_core(core_matrix)
    everything = lax.all_gather(basis_piece, ("row", "col"), axis=0, tiled=True)
    basis_rows = lax.dynamic_slice_in_dim(everything, row_index * block_rows, block_rows, 0)
    basis_cols = lax.dynamic_slice_in_dim(everything, col_index * block_cols, block_cols, 0)
    partial_rows = product(mobility, basis_cols)
    spread_rows = product(lax.psum(partial_rows, "col"), kernel)
    inner_sum = lax.psum(product_tn(basis_rows, spread_rows), "row")
    inner = product_tn(kernel, inner_sum)
    correction_rows = spread_rows - 0.5 * product(basis_rows, inner)
    correction_cols = correction_columns(correction_rows, block_ratio)
    left_side = jnp.concatenate([basis_rows, correction_rows], axis=1)
    right_side = jnp.concatenate([correction_cols, basis_cols], axis=1)
    updated = mobility - product_nt(left_side, right_side)
    return (updated, panel_factor)


def solution(mesh):
    in_specs = (P(("row", "col"), None), P("row", "col"))
    out_specs = (P("row", "col"), P())
    return jax.shard_map(
        on_device, mesh=mesh, in_specs=in_specs, out_specs=out_specs, check_vma=False
    )
```

profile of v0, /device:TPU:1, one launch (start us, length us, event | category | flops | bytes accessed | tf_op | source)
XLA Modules:
  0.0 727.7 jit_solution(3753922273948830282)
XLA Ops:
  7.2 0.7 copy-done
  7.9 0.9 fusion.18
  8.8 0.8 fusion.14
  9.7 249.4 %all-reduce.12.cloned.1.call-done = (f32[128,128]{0,1:T(8,128)}, f32[128,128]{1,0:T(8,128)}) async-done(((f32[128,128]{0,1:T(8,128)}, f32[128,128]{1,0:T(8,128)}), (f32[128,128]{0,1:T(8,128)}, f32[128,128]{1,0:T(8,128)})) %all-reduce.12.cloned.1.call-update) | async-done | bytes 131088 | tf_op jit(solution)/shard_map/psum | solution.py:70
  259.1 0.9 copy.5
  260.0 0.9 fusion.12
  260.9 11.7 %cholesky.19 = f32[128,128]{1,0:T(8,128)S(1)} custom-call(f32[128,128]{1,0:T(8,128)S(1)} %fusion.12), custom_call_target="Cholesky" | custom-call | tf_op jit(solution)/shard_map/jit(cholesky)/cholesky | solution.py:71
  272.6 0.6 compare_reduce_fusion
  273.3 0.7 fusion.15
  273.9 9.8 %custom-call.10 = f32[1,128,128]{1,2,0:T(8,128)S(1)} custom-call(f32[1,128,128]{2,1,0:T(8,128)S(1)} %get-tuple-element.49), custom_call_target="InvertDiagBlocksLowerTriangular" | custom-call | tf_op jit(solution)/shard_map/jit(_solve_triangular)/triangular_solve | solution.py:73
  283.8 0.8 fusion.3
  284.7 1.1 convolution_add_fusion
  285.9 115.3 %all-gather.2.cloned.1.call-done = f32[16384,128]{1,0:T(8,128)} async-done(((f32[64,128]{1,0:T(8,128)}), f32[16384,128]{1,0:T(8,128)}) %all-gather.2.cloned.1.call-update) | async-done | bytes 8388624 | tf_op jit(solution)/shard_map/all_gather | solution.py:78
  401.2 1.3 constant_dynamic-slice_fusion.1
  402.5 7.5 %convolution_bitcast_fusion.1 = f32[1024,128]{0,1:T(8,128)} fusion(f32[1024,128]{1,0:T(8,128)S(1)} %get-tuple-element.47, f32[1024,1024]{1,0:T(8,128)} %param.5), kind=kOutput, calls=%fused_computation.7 | convolution fusion | flops 1610612736 | bytes 5242880 | tf_op jit(solution)/shard_map/dot_general | solution.py:13
  410.2 7.1 while.11
  410.5 0.3 convolution_bitcast_fusion.4
  411.1 0.3 convolution_bitcast_fusion.4
  411.7 0.3 convolution_bitcast_fusion.4
  412.3 0.3 convolution_bitcast_fusion.4
  412.9 0.3 convolution_bitcast_fusion.4
  416.4 0.3 convolution_bitcast_fusion.4
  417.0 0.3 convolution_bitcast_fusion.4
  417.3 83.1 %all-reduce.6.cloned.1.call-done = f32[1024,128]{0,1:T(8,128)} async-done(((f32[1024,128]{0,1:T(8,128)}), f32[1024,128]{0,1:T(8,128)}) %all-reduce.6.cloned.1.call-update) | async-done | bytes 524304 | tf_op jit(solution)/shard_map/psum | solution.py:82
  500.4 1.6 fusion.19
  502.1 1.6 fusion.20
  504.0 99.9 %all-reduce.8.cloned.1.call-done = f32[128,128]{1,0:T(8,128)} async-done(((f32[128,128]{1,0:T(8,128)}), f32[128,128]{1,0:T(8,128)}) %all-reduce.8.cloned.1.call-update) | async-done | bytes 65552 | tf_op jit(solution)/shard_map/psum | solution.py:83
  603.9 1.0 fusion.21
  604.9 1.4 broadcast_select_fusion
  606.3 0.7 copy.9
  607.1 107.4 %all-reduce.10.cloned.1.call-done = f32[1024,128]{1,0:T(8,128)} async-done(((f32[1024,128]{1,0:T(8,128)}), f32[1024,128]{1,0:T(8,128)}) %all-reduce.10.cloned.1.call-update) | async-done | bytes 524304 | tf_op jit(solution)/shard_map/psum | solution.py:9
  714.4 6.7 convolution_subtract_fusion.1
  (45 shorter events, 5.5 us)
Async XLA Ops:
  7.2 0.8 copy-start
  7.2 251.9 %all-reduce.12.cloned.1.call-start = ((), (), s32[]{:S(2)}) async-start(), calls=%async_computation.4 | async-start | bytes 262144 | tf_op jit(solution)/shard_map/psum | solution.py:70
  9.7 391.5 %all-gather.2.cloned.1.call-start = ((), (), s32[]{:S(2)}) async-start(), calls=%async_computation | async-start | bytes 8421376 | tf_op jit(solution)/shard_map/all_gather | solution.py:78
  284.6 215.8 %all-reduce.6.cloned.1.call-start = ((), (), s32[]{:S(2)}) async-start(), calls=%async_computation.1 | async-start | bytes 1048576 | tf_op jit(solution)/shard_map/psum | solution.py:82
  410.0 193.9 %all-reduce.8.cloned.1.call-start = ((), (), s32[]{:S(2)}) async-start(), calls=%async_computation.2 | async-start | bytes 131072 | tf_op jit(solution)/shard_map/psum | solution.py:83
  503.7 210.7 %all-reduce.10.cloned.1.call-start = ((), (), s32[]{:S(2)}) async-start(), calls=%async_computation.3 | async-start | bytes 1048576 | tf_op jit(solution)/shard_map/psum | solution.py:9
Sparse Core Ops, SparseCore 0:
  14.2 244.8 all-reduce.11
  284.7 116.4 all-gather.1
  410.1 90.2 all-reduce.5
  503.8 99.9 all-reduce.7
  606.6 107.7 all-reduce.9
where the time goes:
time: 728 us
  waiting for transfers between devices  655 us (90%)
  matrix products  30.2 us (4%)
  other arithmetic  23.7 us (3%)
  between operations  13.9 us (2%)
    psum x1, waiting for transfers between devices, on_device(): gram_sum, top_rows = lax.psum((gram_term, top_term), ('row', 'col'))  249 us
    all_gather x1, waiting for transfers between devices, on_device(): everything = lax.all_gather(basis_piece, ('row', 'col'), axis=0, tiled=True)  115 us
    psum x1, waiting for transfers between devices, spread(): return lax.psum(jnp.where(mine, shard, jnp.zeros_like(shard)), axis)  107 us
    psum x1, waiting for transfers between devices, on_device(): inner_sum = lax.psum(product_tn(basis_rows, spread_rows), 'row')  99.9 us
    psum x1, waiting for transfers between devices, on_device(): spread_rows = product(lax.psum(partial_rows, 'col'), kernel)  83.1 us
    dot_general x28, matrix products, product(): jnp.dot(first_op, second_op, precision=lax.Precision.HIGHEST, preferred_e...  17.9 us
  transfers between devices with their start and end apart: 5, of which 5 were waited for; matrix products, arithmetic and copies ran while one was open for 1% of the time, Pallas kernels for 0%

commit v1 on v0

--- a/solution.py
+++ b/solution.py
@@ -67,7 +67,7 @@
     )
     gram_term = product_tn(panel, panel)
     top_term = product(selector, panel)
-    gram_sum, top_rows = lax.psum((gram_term, top_term), ("row", "col"))
+    gram_sum, top_rows = jax.lax.psum(jax.lax.psum((gram_term, top_term), "col"), "row")
     lower_factor = jnp.linalg.cholesky(gram_sum)
     panel_factor = lower_factor.T
     ortho_piece = jax.scipy.linalg.solve_triangular(lower_factor, panel.T, lower=True).T

time: 728 us -> 786 us (1.080)
  waiting for transfers between devices: 655 us -> 712 us
    psum x1 -> x3, waiting for transfers between devices: 249 us -> 301 us  [the longest x2 205 us: on_device(): jax.lax.psum(jax.lax.psum((gram_term, top_term), 'col'), 'row')]
  transfers between devices with their start and end apart: 5 -> 7, of which waited for: 5 -> 7; matrix products, arithmetic and copies ran while one was open for 1% -> 0% of each run, Pallas kernels for 0% -> 0%
where the time goes in v1:
time: 786 us; the launch traced here: 785 us
  waiting for transfers between devices  712 us (91%)
  matrix products  30.2 us (4%)
  other arithmetic  23.7 us (3%)
  between operations  14.2 us (2%)
    psum x2, waiting for transfers between devices, on_device(): jax.lax.psum(jax.lax.psum((gram_term, top_term), 'col'), 'row')  205 us
    all_gather x1, waiting for transfers between devices, on_device(): everything = lax.all_gather(basis_piece, ('row', 'col'), axis=0, tiled=True)  116 us
    psum x1, waiting for transfers between devices, spread(): return lax.psum(jnp.where(mine, shard, jnp.zeros_like(shard)), axis)  108 us
    psum x1, waiting for transfers between devices, on_device(): inner_sum = lax.psum(product_tn(basis_rows, spread_rows), 'row')  97.3 us
    psum x1, waiting for transfers between devices, on_device(): jax.lax.psum((gram_term, top_term), 'col')  96.2 us
    psum x1, waiting for transfers between devices, on_device(): spread_rows = product(lax.psum(partial_rows, 'col'), kernel)  90.4 us
    dot_general x28, matrix products, product(): jnp.dot(first_op, second_op, precision=lax.Precision.HIGHEST, preferred_e...  17.9 us
  transfers between devices with their start and end apart: 7, of which 7 were waited for; matrix products, arithmetic and copies ran while one was open for 0% of the time, Pallas kernels for 0%

profile of v1, /device:TPU:1, one launch (start us, length us, event | category | flops | bytes accessed | tf_op | source)
XLA Modules:
  0.0 785.3 jit_solution(9439968328560815604)
XLA Ops:
  7.2 0.7 copy-done
  7.9 0.9 fusion.18
  8.9 96.2 %all-reduce.8.cloned.1.call-done = f32[128,128]{0,1:T(8,128)} async-done(((f32[128,128]{0,1:T(8,128)}), f32[128,128]{0,1:T(8,128)}) %all-reduce.8.cloned.1.call-update) | async-done | bytes 65552 | tf_op jit(solution)/shard_map/psum | solution.py:70
  105.2 102.7 %all-reduce.10.cloned.1.call-done = f32[128,128]{0,1:T(8,128)} async-done(((f32[128,128]{0,1:T(8,128)}), f32[128,128]{0,1:T(8,128)}) %all-reduce.10.cloned.1.call-update) | async-done | bytes 65552 | tf_op jit(solution)/shard_map/psum | solution.py:70
  207.9 0.9 copy.5
  208.8 0.9 fusion.12
  209.7 11.7 %cholesky.19 = f32[128,128]{1,0:T(8,128)S(1)} custom-call(f32[128,128]{1,0:T(8,128)S(1)} %fusion.12), custom_call_target="Cholesky" | custom-call | tf_op jit(solution)/shard_map/jit(cholesky)/cholesky | solution.py:71
  221.4 0.6 compare_reduce_fusion
  222.1 0.7 fusion.15
  222.7 9.8 %custom-call.10 = f32[1,128,128]{1,2,0:T(8,128)S(1)} custom-call(f32[1,128,128]{2,1,0:T(8,128)S(1)} %get-tuple-element.49), custom_call_target="InvertDiagBlocksLowerTriangular" | custom-call | tf_op jit(solution)/shard_map/jit(_solve_triangular)/triangular_solve | solution.py:73
  232.5 0.8 fusion.3
  233.4 0.8 fusion.14
  234.2 116.2 %all-gather.2.cloned.1.call-done = f32[16384,128]{1,0:T(8,128)} async-done(((f32[64,128]{1,0:T(8,128)}), f32[16384,128]{1,0:T(8,128)}) %all-gather.2.cloned.1.call-update) | async-done | bytes 8388624 | tf_op jit(solution)/shard_map/all_gather | solution.py:78
  350.4 1.3 constant_dynamic-slice_fusion.1
  351.7 7.5 convolution_bitcast_fusion.1
  359.2 90.4 %all-reduce.18.cloned.1.call-done = (f32[1024,128]{0,1:T(8,128)}, f32[128,128]{1,0:T(8,128)}) async-done(((f32[1024,128]{0,1:T(8,128)}, f32[128,128]{1,0:T(8,128)}), (f32[1024,128]{0,1:T(8,128)}, f32[128,128]{1,0:T(8,128)})) %all-reduce.18.cloned.1.call-update) | async-done | bytes 589840 | tf_op jit(solution)/shard_map/psum | solution.py:82
  450.0 101.9 %all-reduce.12.cloned.1.call-done = f32[128,128]{1,0:T(8,128)} async-done(((f32[128,128]{1,0:T(8,128)}), f32[128,128]{1,0:T(8,128)}) %all-reduce.12.cloned.1.call-update) | async-done | bytes 65552 | tf_op jit(solution)/shard_map/psum | solution.py:70
  551.9 1.1 convolution_add_fusion
  553.0 7.1 while.11
  553.3 0.3 convolution_bitcast_fusion.4
  553.9 0.3 convolution_bitcast_fusion.4
  554.5 0.3 convolution_bitcast_fusion.4
  555.1 0.3 convolution_bitcast_fusion.4
  555.7 0.3 convolution_bitcast_fusion.4
  560.1 1.6 fusion.19
  561.8 1.6 fusion.20
  563.7 97.3 %all-reduce.14.cloned.1.call-done = f32[128,128]{1,0:T(8,128)} async-done(((f32[128,128]{1,0:T(8,128)}), f32[128,128]{1,0:T(8,128)}) %all-reduce.14.cloned.1.call-update) | async-done | bytes 65552 | tf_op jit(solution)/shard_map/psum | solution.py:83
  661.0 1.0 fusion.21
  662.1 1.4 broadcast_select_fusion
  663.4 0.7 copy.9
  664.2 107.5 %all-reduce.16.cloned.1.call-done = f32[1024,128]{1,0:T(8,128)} async-done(((f32[1024,128]{1,0:T(8,128)}), f32[1024,128]{1,0:T(8,128)}) %all-reduce.16.cloned.1.call-update) | async-done | bytes 524304 | tf_op jit(solution)/shard_map/psum | solution.py:9
  771.7 6.8 convolution_subtract_fusion.1
  (51 shorter events, 6.2 us)
Async XLA Ops:
  7.2 0.8 copy-start
  7.2 98.0 %all-reduce.8.cloned.1.call-start = ((), (), s32[]{:S(2)}) async-start(), calls=%async_computation | async-start | bytes 131072 | tf_op jit(solution)/shard_map/psum | solution.py:70
  8.9 199.0 %all-reduce.10.cloned.1.call-start = ((), (), s32[]{:S(2)}) async-start(), calls=%async_computation.1 | async-start | bytes 131072 | tf_op jit(solution)/shard_map/psum | solution.py:70
  105.2 245.2 %all-gather.2.cloned.1.call-start = ((), (), s32[]{:S(2)}) async-start(), calls=%async_computation.2 | async-start | bytes 8421376 | tf_op jit(solution)/shard_map/all_gather | solution.py:78
  233.4 216.3 %all-reduce.18.cloned.1.call-start = ((), (), s32[]{:S(2)}) async-start(), calls=%async_computation.6 | async-start | bytes 1179648 | tf_op jit(solution)/shard_map/psum | solution.py:82
  359.1 192.7 %all-reduce.12.cloned.1.call-start = ((), (), s32[]{:S(2)}) async-start(), calls=%async_computation.3 | async-start | bytes 131072 | tf_op jit(solution)/shard_map/psum | solution.py:70
  449.7 211.3 %all-reduce.14.cloned.1.call-start = ((), (), s32[]{:S(2)}) async-start(), calls=%async_computation.4 | async-start | bytes 131072 | tf_op jit(solution)/shard_map/psum | solution.py:83
  563.4 208.3 %all-reduce.16.cloned.1.call-start = ((), (), s32[]{:S(2)}) async-start(), calls=%async_computation.5 | async-start | bytes 1048576 | tf_op jit(solution)/shard_map/psum | solution.py:9
Sparse Core Ops, SparseCore 0:
  11.8 93.3 all-reduce.7
  107.6 100.2 all-reduce.9
  233.5 116.8 all-gather.1
  359.3 90.3 all-reduce.17
  451.8 100.0 all-reduce.11
  563.5 97.4 all-reduce.13
  663.9 107.7 all-reduce.15
